TPU v7x, 256 devices: a whole 4x4x8 slice. The times are simulated.
256 devices in a mesh: grp: 4 (over z_lo, core), wide: 64 (over y, x, z_hi).
Axes of the slice: x: 4, y: 4, z: 8 (z_hi: 4, z_lo: 2; z = z_hi * 2 + z_lo), core: 2. Of those that a mesh axis runs over, the one named last changes fastest.
Arguments:
- acts: float32 [16384, 2048], P('wide'), may hold values from -6 to 6
- dec_bias: float32 [2048], replicated, may hold values from -2 to 2
- enc_weight: bfloat16 [4096, 2048], P(('grp', 'wide')), may hold values from -0.125 to 0.125
- enc_bias: bfloat16 [4096], P(('grp', 'wide')), may hold values from -3 to 3
- dec_weight: bfloat16 [4096, 2048], P(('grp', 'wide')), may hold values from -0.09375 to 0.09375
Outputs:
- recon: bfloat16 [16384, 2048], P('wide')
- grad_enc: float32 [4096, 2048], P(('grp', 'wide'))
- grad_dec: float32 [4096, 2048], P(('grp', 'wide'))
- grad_bias: float32 [4096], P(('grp', 'wide'))
All inputs are finite; a program needn't handle non-finite values.
Results may differ from a plain program's by a relative error of at most 0.0055.
Values may be sent and summed in bfloat16 or wider, within the bound.
A program may use at most 64 MiB of HBM per device.

v0:
```python
import jax
import jax.numpy as jnp
from jax import lax
from jax.sharding import Mesh
from jax.sharding import PartitionSpec as P

GRP = ("grp_0", "grp_1")
GRP_WIDE = ("grp_0", "grp_1", "wide")


sparsity_weight = 0.5


def split_up(shard, dim, devices):
    before, after = (shard.shape[:dim], shard.shape[dim + 1 :])
    return jnp.moveaxis(shard.reshape(*before, devices, -1, *after), dim, 0)


def sum_at_owner(shard, axis, dim):
    tiles = split_up(shard, dim, lax.axis_size(axis))
    arrived = lax.all_to_all(tiles, axis, split_axis=0, concat_axis=0, tiled=True)
    return arrived.sum(axis=0)


def joined_along(tiles, dim):
    tiles = jnp.moveaxis(tiles, 0, dim)
    shape = tiles.shape
    return tiles.reshape(*shape[:dim], shape[dim] * shape[dim + 1], *shape[dim + 2 :])


def gather_in_order(shard, axes, sequence):
    tiles = shard[None]
    for k in sequence:
        tiles = lax.all_gather(tiles, axes[k], axis=0, tiled=True)
    carried = [lax.axis_size(axes[k]) for k in reversed(sequence)]
    tiles = tiles.reshape(*carried, *shard.shape)
    turned = sorted(range(len(sequence)), key=lambda place: sequence[len(sequence) - 1 - place])
    return tiles.transpose(*turned, *range(len(sequence), tiles.ndim)).reshape(-1, *shard.shape)


def gather_axes(shard, axes, sequence, dim):
    return joined_along(gather_in_order(shard, axes, sequence), dim)


def in_one_piece(arrays, axis, dim, along):
    columns = [a.reshape(*a.shape[:along], -1) for a in arrays]
    both = jnp.concatenate(columns, axis=along)
    whole, at, done = (lax.psum_scatter(both, axis, scatter_dimension=dim, tiled=True), 0, [])
    for a, column in zip(arrays, columns):
        piece = whole[..., at : at + column.shape[along]]
        done.append(piece.reshape(*piece.shape[:along], *a.shape[along:]))
        at += column.shape[along]
    return tuple(done)


def encode_rows(centered, pieces):
    enc_rows, enc_shift = pieces
    pre = lax.dot_general(
        centered, enc_rows, (((1,), (1,)), ((), ())), preferred_element_type=jnp.float32
    )
    return pre + enc_shift.astype(jnp.float32)[None, :]


def per_device(acts, dec_bias, enc_weight, enc_bias, dec_weight):
    total_rows = acts.shape[0] * lax.axis_size("wide")
    scale = total_rows ** (-0.5)
    centered = (acts - dec_bias[None, :]).astype(jnp.bfloat16)
    pre_acts = encode_rows(
        centered, lax.all_gather((enc_weight, enc_bias), "wide", axis=0, tiled=True)
    )
    codes_bf = jnp.maximum(pre_acts, 0.0).astype(jnp.bfloat16)
    dec_group = lax.all_gather(dec_weight, "wide", axis=0, tiled=True)
    partial_value = jnp.dot(codes_bf, dec_group, preferred_element_type=jnp.float32)
    share = sum_at_owner(partial_value, GRP, 1)
    width = share.shape[1]
    offset = lax.axis_index(GRP) * width
    bias_part = lax.dynamic_slice_in_dim(dec_bias, offset, width, 0)
    acts_part = lax.dynamic_slice_in_dim(acts, offset, width, 1)
    full_part = share + bias_part[None, :]
    recon, error = (
        gather_axes(full_part.astype(jnp.bfloat16), GRP, (0, 1), 1),
        gather_axes((full_part - acts_part).astype(jnp.bfloat16), GRP, (0, 1), 1),
    )
    codes = jnp.maximum(pre_acts, 0.0)
    codes_again = codes.astype(jnp.bfloat16)
    dec_float = dec_group.astype(jnp.float32)
    norms = jnp.sqrt(jnp.sum(dec_float * dec_float, axis=1) + 1e-06)
    back = lax.dot_general(
        error, dec_group, (((1,), (1,)), ((), ())), preferred_element_type=jnp.float32
    )
    grad_pre = jnp.where(pre_acts > 0.0, back + sparsity_weight * norms[None, :], 0.0)
    grad_pre_bf = grad_pre.astype(jnp.bfloat16)
    data_term = lax.dot_general(
        codes_again, error, (((0,), (0,)), ((), ())), preferred_element_type=jnp.float32
    )
    col_sums = jnp.sum(codes, axis=0)
    term_dec = scale * (
        data_term + sparsity_weight * col_sums[:, None] * dec_float / norms[:, None]
    )
    term_enc = scale * lax.dot_general(
        grad_pre_bf, centered, (((0,), (0,)), ((), ())), preferred_element_type=jnp.float32
    )
    term_bias = scale * jnp.sum(grad_pre, axis=0)
    grad_enc, grad_dec, grad_bias = in_one_piece((term_enc, term_dec, term_bias), "wide", 0, 1)
    return (recon, grad_enc, grad_dec, grad_bias)


def solution(mesh):
    torus = Mesh(mesh.devices.reshape(2, 2, mesh.shape["wide"]), ("grp_0", "grp_1", "wide"))
    placed = (P("wide", None), P(), P(GRP_WIDE, None), P(GRP_WIDE), P(GRP_WIDE, None))
    return jax.shard_map(
        per_device,
        mesh=torus,
        in_specs=placed,
        out_specs=(P("wide", None), P(GRP_WIDE, None), P(GRP_WIDE, None), P(GRP_WIDE)),
        check_vma=False,
    )
```

profile of v0, /device:TPU:1, one launch (start us, length us, event | category | flops | bytes accessed | tf_op | source)
XLA Modules:
  0.0 584.2 jit_solution(3712044903776946574)
XLA Ops:
  7.9 0.7 all-gather.8.cloned.1.call-update
  8.7 1.3 dynamic-slice
  10.6 0.8 dynamic-update-slice
  11.4 175.9 %all-reduce = bf16[1024]{0:T(1024)(128)(2,1)S(1)} all-reduce(bf16[1024]{0:T(1024)(128)(2,1)S(1)} %dynamic-update-slice), channel_id=1, replica_groups=mesh['grp_0'=2,'grp_1'=2,'wide'=64] {'wide'}, use_global_device_ids=true, to_apply=%add | all-reduce | flops 1024 | bytes 4096
  187.4 4.2 maximum_reduce_fusion
  191.6 4.0 all-gather.8.cloned.1.call-done
  195.7 3.4 fusion.7
  199.1 1.5 copy.34
  200.7 28.5 %all-to-all-start = ((f32[4,256,512]{2,1,0:T(8,128)}), f32[4,256,512]{2,1,0:T(8,128)S(1)}, u32[]{:S(2)}, u32[]{:S(2)}) async-start(f32[4,256,512]{2,1,0:T(8,128)} %bitcast.35), calls=%async_computation | async-start | bytes 4194304 | tf_op jit(solution)/shard_map/all_to_all | solution.py:21
  229.2 24.6 %all-to-all-done = f32[4,256,512]{2,1,0:T(8,128)S(1)} async-done(((f32[4,256,512]{2,1,0:T(8,128)}), f32[4,256,512]{2,1,0:T(8,128)S(1)}, u32[]{:S(2)}, u32[]{:S(2)}) %all-to-all-start) | async-done | bytes 2097184 | tf_op jit(solution)/shard_map/all_to_all | solution.py:21
  254.1 1.2 subtract_convert_fusion.1
  255.2 7.7 %all-gather = bf16[512,512]{1,0:T(8,128)(2,1)} all-gather(bf16[256,512]{1,0:T(8,128)(2,1)S(1)} %subtract_convert_fusion.1), channel_id=2, replica_groups=mesh['grp_0'=2,'grp_1'=2,'wide'=64] {'grp_0'}, dimensions={0}, use_global_device_ids=true | all-gather | bytes 786432 | tf_op jit(solution)/shard_map/all_gather | solution.py:34
  263.0 3.1 fusion
  266.2 6.9 %all_gather.24 = bf16[2,256,512]{2,1,0:T(8,128)(2,1)} all-gather(bf16[1,256,512]{2,1,0:T(8,128)(2,1)S(1)} %fusion.5), channel_id=1, replica_groups=mesh['grp_0'=2,'grp_1'=2,'wide'=64] {'grp_0'}, dimensions={0}, use_global_device_ids=true | all-gather | bytes 786432 | tf_op jit(solution)/shard_map/all_gather | solution.py:34
  273.2 1.3 copy.28
  275.0 3.7 fusion.11
  278.7 4.5 convolution_multiply_fusion
  283.5 4.7 fusion.3
  288.7 6.2 %pad_maximum_fusion = f32[1024,4097]{1,0:T(8,128)} fusion(f32[1024,1]{1,0:T(8,128)S(1)} %copy.30, f32[1024,2048]{1,0:T(8,128)S(1)} %fusion.3, f32[1024,2048]{1,0:T(8,128)S(1)} %copy-done), kind=kLoop, calls=%fused_computation | loop fusion | flops 8390656 | bytes 33562624 | tf_op jit(solution)/shard_map/concatenate | solution.py:47
  294.9 1.3 copy.26
  296.8 1.4 copy.31
  298.2 276.5 %reduce-scatter.2.cloned.1.call-done = f32[16,4097]{1,0:T(8,128)} async-done(((f32[1024,4097]{1,0:T(8,128)}), f32[16,4097]{1,0:T(8,128)}) %reduce-scatter.2.cloned.1.call-update) | async-done | bytes 262224 | tf_op jit(solution)/shard_map/reduce_scatter | solution.py:48
  574.7 1.7 fusion.10
  576.4 1.3 slice_reduce_fusion
  (33 shorter events, 3.1 us)
Async XLA Ops:
  7.2 180.2 %all-gather.6.cloned.1.call-start = ((), (), s32[]{:S(2)}) async-start(), calls=%async_computation.2 | async-start | bytes 4259840 | tf_op jit(solution)/shard_map/all_gather | solution.py:69
  7.9 187.8 %all-gather.8.cloned.1.call-start = ((), (), s32[]{:S(2)}) async-start(), calls=%async_computation.3 | async-start | bytes 4259840 | tf_op jit(solution)/shard_map/all_gather | solution.py:72
  191.6 9.0 %copy-start.2 = (f32[256,1024]{1,0:T(8,128)}, f32[256,1024]{1,0:T(8,128)S(1)}, u32[]{:S(2)}) copy-start(f32[256,1024]{1,0:T(8,128)S(1)} %get-tuple-element.15) | copy-start | bytes 3145732
  199.1 30.0 %copy-start.4 = (f32[2048]{0:T(1024)S(1)}, f32[2048]{0:T(1024)}, u32[]{:S(2)}) copy-start(f32[2048]{0:T(1024)} %param.6) | copy-start | bytes 24580
  200.7 53.2 %all-to-all-start = ((f32[4,256,512]{2,1,0:T(8,128)}), f32[4,256,512]{2,1,0:T(8,128)S(1)}, u32[]{:S(2)}, u32[]{:S(2)}) async-start(f32[4,256,512]{2,1,0:T(8,128)} %bitcast.35), calls=%async_computation | async-start | bytes 4194304 | tf_op jit(solution)/shard_map/all_to_all | solution.py:21
  229.1 44.0 %all-gather.12.cloned.1.call-start = ((), (), s32[]{:S(2)}) async-start(), calls=%async_computation.5 | async-start | bytes 1572864 | tf_op jit(solution)/shard_map/all_gather | solution.py:34
  262.9 32.0 %all-gather.10.cloned.1.call-start = ((), (), s32[]{:S(2)}) async-start(), calls=%async_computation.4 | async-start | bytes 1572864 | tf_op jit(solution)/shard_map/all_gather | solution.py:34
  266.1 9.0 %copy-start.3 = (f32[256,1024]{1,0:T(8,128)S(1)}, f32[256,1024]{1,0:T(8,128)}, u32[]{:S(2)}) copy-start(f32[256,1024]{1,0:T(8,128)} %copy-done.2) | copy-start | bytes 3145732
  273.1 301.6 %reduce-scatter.2.cloned.1.call-start = ((), (), s32[]{:S(2)}) async-start(), calls=%async_computation.6 | async-start | bytes 17571840 | tf_op jit(solution)/shard_map/reduce_scatter | solution.py:48
  275.0 3.7 copy-start.1
  283.5 5.2 copy-start
Sparse Core Ops, SparseCore 0:
  11.3 93.3 all-gather.5
  108.0 87.5 all-gather.7
  263.1 7.6 all-gather.11
  273.2 14.8 all-gather.9
  295.0 279.5 reduce-scatter.1
where the time goes:
time: 586 us; the launch traced here: 584 us
  waiting for transfers between devices  307 us (52%)
  blocking collectives  191 us (33%)
  starting transfers between devices  28.6 us (5%)
  matrix products  20.5 us (3%)
  between operations  14.6 us (2%)
  local copies, waits for them, and re-layouts  12.5 us (2%)
  other arithmetic  10.8 us (2%)
    reduce_scatter x1, waiting for transfers between devices, in_one_piece(): lax.psum_scatter(both, axis, scatter_dimension=dim, tiled=True)  276 us
    unnamed x1, blocking collectives  176 us
    all_to_all x1, starting transfers between devices, sum_at_owner(): lax.all_to_all(tiles, axis, split_axis=0, concat_axis=0, tiled=True)  28.5 us
    all_to_all x1, waiting for transfers between devices, sum_at_owner(): lax.all_to_all(tiles, axis, split_axis=0, concat_axis=0, tiled=True)  24.6 us
    all_gather x2, blocking collectives, gather_in_order(): tiles = lax.all_gather(tiles, axes[k], axis=0, tiled=True)  14.6 us
  transfers between devices with their start and end apart: 6, of which 3 were waited for; matrix products, arithmetic and copies ran while one was open for 6% of the time, Pallas kernels for 0%

commit v1 on v0

v1 whole, which is shorter than its diff:
```python
import jax
import jax.numpy as jnp
from jax import lax
from jax.experimental import pallas as pl
from jax.experimental.pallas import tpu as pltpu
from jax.sharding import Mesh
from jax.sharding import PartitionSpec as P


AXES = ("zl", "c", "y", "x", "h")
MESH = pl.DeviceIdType.MESH
F32, BF16 = jnp.float32, jnp.bfloat16
SPARSITY = 0.5
NZ, SIDE, ROWS, D, OWN, LAT = 8, 4, 256, 2048, 16, 256
PORTION = ROWS // 2
SUB = PORTION // 2
CH = SUB // 2
WE = D + 128
GE = D + 256
TILE = 512


class Semaphores:
    def __init__(self):
        self.names = {}

    def __call__(self, *name):
        return self.names.setdefault(name, len(self.names))


N_SEMS = 128
NT = (((1,), (1,)), ((), ()))


def kernel(
    acts, dbias, encb, dec, recon, genc, gdec, gbias,
    cent, wenc, wdec, codes, codes_t, pown, psend, precv, psum, rsp, rsm, err, acc_e, acc_d, gb, cs,
    pay_e, pay_d, e_far, e_near, tot_e, e_last, d_far, d_near, tot_d, d_last, rec, ssem, rsem,
):
    zl, c, y, x, h = [lax.axis_index(a) for a in AXES]
    z = 2 * h + zl
    sems = Semaphores()
    pending = []

    def wrap(v, n):
        return lax.rem(v + 2 * n, n)

    def at_z(dz):
        q = wrap(z + dz, NZ)
        return (lax.rem(q, 2), c, y, x, lax.div(q, 2))

    def at_y(dy):
        return (zl, c, wrap(y + dy, SIDE), x, h)

    def at_x(dx):
        return (zl, c, y, wrap(x + dx, SIDE), h)

    partner = (zl, 1 - c, y, x, h)
    pair = (1 - zl, c, y, x, h)

    def copy(src, dst, sem, dev):
        return pltpu.make_async_remote_copy(
            src_ref=src, dst_ref=dst, send_sem=ssem.at[sem], recv_sem=rsem.at[sem], device_id=dev, device_id_type=MESH
        )

    def send(src, dst, sem, dev):
        cp = copy(src, dst, sem, dev)
        cp.start()
        pending.append(cp)

    def arrive(dst, sem):
        copy(dst, dst, sem, partner).wait_recv()

    def rows(ref, p, k, core=None):
        who = c if core is None else core
        return ref.at[p, pl.ds(pl.multiple_of(who * SUB + k * CH, CH), CH)]

    barrier = pltpu.get_barrier_semaphore()
    friends = [partner, at_z(1), at_z(-1)] + [at_y(d) for d in (1, 2, 3)] + [at_x(d) for d in (1, 2, 3)]
    for f in friends:
        pl.semaphore_signal(barrier, inc=1, device_id=f, device_id_type=MESH)
    pl.semaphore_wait(barrier, len(friends))

    for d in (1, 2, 3):
        send(encb, wenc.at[y, x], sems("we1", d), at_x(d))
        send(dec, wdec.at[y, x], sems("wd1", d), at_y(d))

    for q in range(2):
        cent[2 * h + q] = (acts[q * PORTION : (q + 1) * PORTION] - dbias[...]).astype(BF16)
    up = [wrap(2 * h + o, NZ) for o in (-2, -1, -4)]
    down = [wrap(2 * h + o, NZ) for o in (3, 2, 5)]
    for j in range(3):
        for k in range(2):
            sems("ap", j, k), sems("am", j, k)

    def piece(p, k):
        return rows(cent, p, k)

    for j in range(2):
        for k in range(2):
            @pl.when(zl == 1)
            def _(j=j, k=k):
                copy(piece(2 * h + j, k), piece(2 * h + j, k), sems("ap", j, k), at_z(1)).start()

            @pl.when(zl == 0)
            def _(j=j, k=k):
                copy(piece(2 * h + 1 - j, k), piece(2 * h + 1 - j, k), sems("am", j, k), at_z(-1)).start()

    wenc[y, x] = encb[...]
    wdec[y, x] = dec[...]

    def relay_acts(j, k):
        for name, at, dz, first in (("ap", up, 1, 0), ("am", down, -1, 1)):
            part = piece(at[j], k)
            arrive(part, sems(name, j, k))

            @pl.when(zl == first)
            def _():
                copy(part, part, sems(name, j, k), at_z(dz)).start()

            if j == 0:
                @pl.when(zl != first)
                def _():
                    copy(part, part, sems(name, 2, k), at_z(dz)).start()

            send(part, part, sems(name + "c", j, k), partner)

    def from_partner(j):
        for name, at in (("ap", up), ("am", down)):
            for k in range(2):
                arrive(rows(cent, at[j], k, 1 - c), sems(name + "c", j, k))

    relay_acts(0, 0)
    for d in (1, 2, 3):
        arrive(wenc.at[y, wrap(x - d, SIDE)], sems("we1", d))
        arrive(wdec.at[wrap(y - d, SIDE), x], sems("wd1", d))
    for s in (1, -1):
        send(wenc.at[y], wenc.at[y], sems("we2", s), at_y(s))
        send(wdec.at[:, x], wdec.at[:, x], sems("wd2", s), at_x(s))
    relay_acts(0, 1)
    relay_acts(1, 0)
    for s in (1, -1):
        half = pl.ds(0 if s == 1 else 2, 2)
        yn, xn = wrap(y - s, SIDE), wrap(x - s, SIDE)
        arrive(wenc.at[yn], sems("we2", s))
        send(wenc.at[yn, half], wenc.at[yn, half], sems("we3", s), at_y(s))
        arrive(wdec.at[:, xn], sems("wd2", s))
        send(wdec.at[half, xn], wdec.at[half, xn], sems("wd3", s), at_x(s))
    relay_acts(1, 1)
    relay_acts(2, 0)
    for s in (1, -1):
        half = pl.ds(0 if s == 1 else 2, 2)
        arrive(wenc.at[wrap(y + 2, SIDE), half], sems("we3", s))
        arrive(wdec.at[half, wrap(x + 2, SIDE)], sems("wd3", s))

    def encode(b):
        block = cent[pl.ds(2 * b, 2)].reshape(ROWS, D)
        weights = wenc[:, :, :, :D].reshape(LAT, D)
        shift = wenc[:, :, :, D:].reshape(LAT, 128).astype(F32)
        pre = lax.dot_general(weights, block, NT, preferred_element_type=F32)
        value = jnp.maximum(pre + jnp.concatenate([shift, shift], axis=1), 0.0)
        turned = value.T.astype(BF16)
        for q in range(2):
            for who in range(2):
                codes[b, who, q * SUB : (q + 1) * SUB] = turned[q * PORTION + who * SUB : q * PORTION + (who + 1) * SUB]
        codes_t[b] = value.astype(BF16)
        return value[:, :128] + value[:, 128:]

    def decode(b, order):
        for t in range(0, D, TILE):
            right = wdec[:, :, :, t : t + TILE].reshape(LAT, TILE)
            other = jnp.dot(codes[b, 1 - c], right, preferred_element_type=F32).astype(BF16)
            mine = jnp.dot(codes[b, c], right, preferred_element_type=F32)
            for q in range(2):
                psend[2 * b + q, :, t : t + TILE] = other[q * SUB : (q + 1) * SUB]
                pown[2 * b + q, :, t : t + TILE] = mine[q * SUB : (q + 1) * SUB]
        for q in range(2):
            send(psend.at[2 * b + q], precv.at[2 * b + q], sems("px", order, q), partner)

    near = 1 - 2 * zl
    blocks = [h, wrap(h - near, SIDE), wrap(h + near, SIDE), wrap(h + 2, SIDE)]
    cs[...] = encode(blocks[0])
    relay_acts(2, 1)
    decode(blocks[0], 0)
    from_partner(0)
    from_partner(1)
    for i in (1, 2):
        cs[...] += encode(blocks[i])
        decode(blocks[i], i)
    from_partner(2)
    cs[...] += encode(blocks[3])
    decode(blocks[3], 3)

    for i in range(4):
        for q in range(2):
            arrive(precv.at[2 * blocks[i] + q], sems("px", i, q))

    def part_sum(p, k):
        r = slice(k * CH, (k + 1) * CH)
        return pown[p, r] + precv[p, r].astype(F32)

    def pass_on(s, sign, k, with_recv):
        buf, name = (rsp, "rp") if sign == 1 else (rsm, "rm")
        r = slice(k * CH, (k + 1) * CH)
        p = wrap(z + sign * (4 - s), NZ)
        total = part_sum(p, k)
        if with_recv:
            arrive(buf.at[s - 1, r], sems(name, s - 1, k))
            total = total + buf[s - 1, r].astype(F32)
        psum[p, r] = total.astype(BF16)
        send(psum.at[p, r], buf.at[s, r], sems(name, s, k), at_z(sign))

    pass_on(0, 1, 0, False)
    pass_on(0, -1, 1, False)
    pass_on(1, 1, 1, False)
    pass_on(1, -1, 0, False)
    pass_on(1, 1, 0, True)
    pass_on(1, -1, 1, True)
    for s in (2, 3):
        for k in range(2):
            pass_on(s, 1, 1 - k, True)
            pass_on(s, -1, k, True)

    norms = []
    for q in range(2):
        rows_q = wdec[2 * q : 2 * q + 2].reshape(LAT // 2, D).astype(F32)
        norms.append(jnp.sqrt(jnp.sum(rows_q * rows_q, axis=1, keepdims=True) + 1e-06))
    norms = jnp.concatenate(norms, axis=0)

    own_rows = zl * PORTION + c * SUB
    for k in range(2):
        r = slice(k * CH, (k + 1) * CH)
        here = pl.ds(pl.multiple_of(own_rows + k * CH, CH), CH)
        total = part_sum(z, k)
        arrive(rsp.at[3, r], sems("rp", 3, k))
        arrive(rsm.at[3, r], sems("rm", 3, k))
        full = total + rsp[3, r].astype(F32) + rsm[3, r].astype(F32) + dbias[...]
        rec[here] = full.astype(BF16)
        err[z, pl.ds(pl.multiple_of(c * SUB + k * CH, CH), CH)] = (full - acts[here]).astype(BF16)
        mine = rows(err, z, k)
        send(mine, mine, sems("gp", 0, k), at_z(1))
        send(mine, mine, sems("gm", 0, k), at_z(-1))
        send(mine, mine, sems("go", k), partner)

    def relay_err(s):
        for k in range(2):
            for sign, name in ((1, "gp"), (-1, "gm")):
                kept = 0 if sign == 1 else 1
                if s == 3 and k != kept:
                    continue
                part = rows(err, wrap(z - sign * (s + 1), NZ), k)
                arrive(part, sems(name, s, k))
                if s < 2 or (s == 2 and k == kept):
                    send(part, part, sems(name, s + 1, k), at_z(sign))
                send(part, part, sems(name + "c", s, k), partner)

    def err_from_partner(s):
        for k in range(2):
            for sign, name in ((1, "gp"), (-1, "gm")):
                kept = 0 if sign == 1 else 1
                if s == 3 and k != kept:
                    continue
                arrive(rows(err, wrap(z - sign * (s + 1), NZ), k, 1 - c), sems(name + "c", s, k))

    def backward(b, first, last):
        block = err[pl.ds(2 * b, 2)].reshape(ROWS, D)
        weights = wdec[...].reshape(LAT, D)
        back = lax.dot_general(weights, block, NT, preferred_element_type=F32)
        kept = codes_t[b]
        grad_pre = jnp.where(kept.astype(F32) > 0.0, back + SPARSITY * norms, 0.0)
        folded = grad_pre[:, :128] + grad_pre[:, 128:]
        gb[...] = folded if first else gb[...] + folded
        grad_bf = grad_pre.astype(BF16)
        for left, data, acc, pay in ((grad_bf, cent, acc_e, pay_e), (kept, err, acc_d, pay_d)):
            for t in range(0, D, TILE):
                right = data[pl.ds(2 * b, 2), :, t : t + TILE].reshape(ROWS, TILE)
                total = jnp.dot(left, right, preferred_element_type=F32)
                if not first:
                    total = total + acc[:, t : t + TILE]
                if last:
                    pay[:, :, :, t : t + TILE] = total.astype(BF16).reshape(SIDE, SIDE, OWN, TILE)
                else:
                    acc[:, t : t + TILE] = total
            if last and pay is pay_e:
                pay[:, :, :, D : D + 128] = gb[...].astype(BF16).reshape(SIDE, SIDE, OWN, 128)
                pay[:, :, :, D + 128 :] = cs[...].astype(BF16).reshape(SIDE, SIDE, OWN, 128)
            if last:
                (start_e if pay is pay_e else start_d)()

    low, high = pl.ds(0, 2), pl.ds(2, 2)

    def e_part(yy, half):
        return pay_e.at[yy, half]

    def d_part(xx, half):
        return pay_d.at[half, xx]

    def start(part, v, far, close, name, at):
        send(part(wrap(v + 2, SIDE), low), far.at[0], sems(name, "far", 1), at(1))
        send(part(wrap(v + 2, SIDE), high), far.at[1], sems(name, "far", -1), at(-1))
        send(part(wrap(v + 1, SIDE), high), close.at[0, high], sems(name, "own", 1), at(1))
        send(part(wrap(v - 1, SIDE), low), close.at[1, low], sems(name, "own", -1), at(-1))

    def start_e():
        start(e_part, y, e_far, e_near, "e", at_y)

    def start_d():
        start(d_part, x, d_far, d_near, "d", at_x)

    def forward_sum(part, v, far, close, name, at):
        for i, s, half in ((0, 1, low), (1, -1, high)):
            arrive(far.at[i], sems(name, "far", s))
            block = part(wrap(v + s, SIDE), half)
            block[...] = (block[...].astype(F32) + far[i].astype(F32)).astype(BF16)
            send(block, close.at[i, half], sems(name, "sum", s), at(s))

    def at_owner(part, v, w, close, tot, last, name, at):
        for i, s, summed, plain in ((0, 1, low, high), (1, -1, high, low)):
            arrive(close.at[i, plain], sems(name, "own", s))
            arrive(close.at[i, summed], sems(name, "sum", s))
        tot[...] = (
            part(v, pl.ds(0, SIDE))[...].astype(F32) + close[0].astype(F32) + close[1].astype(F32)
        ).astype(BF16)
        for d in (1, 2, 3):
            send(tot.at[wrap(w + d, SIDE)], last.at[d - 1], sems(name, "last", d), at(d))

    def owned(w, tot, last, name):
        total = tot[w].astype(F32)
        for d in (1, 2, 3):
            arrive(last.at[d - 1], sems(name, "last", d))
            total = total + last[d - 1].astype(F32)
        return total

    relay_err(0)
    for k in range(2):
        arrive(rows(err, z, k, 1 - c), sems("go", k))
    err_from_partner(0)
    backward(blocks[0], True, False)
    relay_err(1)
    err_from_partner(1)
    backward(blocks[1], False, False)
    relay_err(2)
    err_from_partner(2)
    backward(blocks[2], False, False)
    relay_err(3)
    own_rec = rec.at[pl.ds(pl.multiple_of(own_rows, SUB), SUB)]
    send(own_rec, own_rec, sems("ro"), partner)
    send(own_rec, own_rec, sems("rz"), pair)
    err_from_partner(3)
    backward(blocks[3], False, True)

    forward_sum(e_part, y, e_far, e_near, "e", at_y)
    forward_sum(d_part, x, d_far, d_near, "d", at_x)
    pair_rec = rec.at[pl.ds(pl.multiple_of((1 - zl) * PORTION + c * SUB, SUB), SUB)]
    arrive(pair_rec, sems("rz"))
    send(pair_rec, pair_rec, sems("rzc"), partner)
    at_owner(e_part, y, x, e_near, tot_e, e_last, "e", at_x)
    at_owner(d_part, x, y, d_near, tot_d, d_last, "d", at_y)
    arrive(rec.at[pl.ds(pl.multiple_of(zl * PORTION + (1 - c) * SUB, SUB), SUB)], sems("ro"))
    arrive(rec.at[pl.ds(pl.multiple_of((1 - zl) * PORTION + (1 - c) * SUB, SUB), SUB)], sems("rzc"))
    recon[...] = rec[...]

    scale = (ROWS * SIDE * SIDE * SIDE) ** -0.5
    total = owned(x, tot_e, e_last, "e")
    genc[...] = scale * total[:, :D]
    gbias[...] = jnp.broadcast_to(scale * jnp.sum(total[:, D : D + 128], axis=1, keepdims=True), (OWN, 128))
    col_sums = jnp.sum(total[:, D + 128 :], axis=1, keepdims=True)
    mine = dec[...].astype(F32)
    own_norms = jnp.sqrt(jnp.sum(mine * mine, axis=1, keepdims=True) + 1e-06)
    total = owned(y, tot_d, d_last, "d")
    gdec[...] = scale * (total + SPARSITY * col_sums * mine / own_norms)

    for name, at, dz in (("ap", up, 1), ("am", down, -1)):
        for j in range(3):
            for k in range(2):
                copy(piece(at[j], k), piece(at[j], k), sems(name, j, k), at_z(dz)).wait_send()
    for cp in pending:
        cp.wait_send()


def per_device(acts, dec_bias, enc_weight, enc_bias, dec_weight):
    encb = jnp.concatenate([enc_weight, jnp.broadcast_to(enc_bias[:, None], (OWN, 128))], axis=1)
    vmem = pl.BlockSpec(memory_space=pltpu.VMEM)
    recon, genc, gdec, gbias = pl.pallas_call(
        kernel,
        name="step",
        out_shape=(
            jax.ShapeDtypeStruct((ROWS, D), BF16),
            jax.ShapeDtypeStruct((OWN, D), F32),
            jax.ShapeDtypeStruct((OWN, D), F32),
            jax.ShapeDtypeStruct((OWN, 128), F32),
        ),
        in_specs=[vmem] * 4,
        out_specs=(vmem,) * 4,
        scratch_shapes=[
            pltpu.VMEM((NZ, PORTION, D), BF16),
            pltpu.VMEM((SIDE, SIDE, OWN, WE), BF16),
            pltpu.VMEM((SIDE, SIDE, OWN, D), BF16),
            pltpu.VMEM((SIDE, 2, PORTION, LAT), BF16),
            pltpu.VMEM((SIDE, LAT, ROWS), BF16),
            pltpu.VMEM((NZ, SUB, D), F32),
            pltpu.VMEM((NZ, SUB, D), BF16),
            pltpu.VMEM((NZ, SUB, D), BF16),
            pltpu.VMEM((NZ, SUB, D), BF16),
            pltpu.VMEM((4, SUB, D), BF16),
            pltpu.VMEM((4, SUB, D), BF16),
            pltpu.VMEM((NZ, PORTION, D), BF16),
            pltpu.VMEM((LAT, D), F32),
            pltpu.VMEM((LAT, D), F32),
            pltpu.VMEM((LAT, 128), F32),
            pltpu.VMEM((LAT, 128), F32),
            pltpu.VMEM((SIDE, SIDE, OWN, GE), BF16),
            pltpu.VMEM((SIDE, SIDE, OWN, D), BF16),
            pltpu.VMEM((2, 2, OWN, GE), BF16),
            pltpu.VMEM((2, SIDE, OWN, GE), BF16),
            pltpu.VMEM((SIDE, OWN, GE), BF16),
            pltpu.VMEM((3, OWN, GE), BF16),
            pltpu.VMEM((2, 2, OWN, D), BF16),
            pltpu.VMEM((2, SIDE, OWN, D), BF16),
            pltpu.VMEM((SIDE, OWN, D), BF16),
            pltpu.VMEM((3, OWN, D), BF16),
            pltpu.VMEM((ROWS, D), BF16),
            pltpu.SemaphoreType.DMA((N_SEMS,)),
            pltpu.SemaphoreType.DMA((N_SEMS,)),
        ],
        compiler_params=pltpu.CompilerParams(collective_id=0, has_side_effects=True, vmem_limit_bytes=60 << 20),
    )(acts, dec_bias[None, :], encb, dec_weight)
    return recon, genc, gdec, gbias[:, 0]


def solution(mesh):
    torus = Mesh(mesh.devices.reshape(2, 2, SIDE, SIDE, SIDE), AXES)
    wide = P(("y", "x", "h"), None)
    return jax.shard_map(
        per_device,
        mesh=torus,
        in_specs=(wide, P(), P(AXES, None), P(AXES), P(AXES, None)),
        out_specs=(wide, P(AXES, None), P(AXES, None), P(AXES)),
        check_vma=False,
    )
```

time: 586 us -> 150 us (0.26)
  waiting for transfers between devices: 307 us -> 0 us
  blocking collectives: 191 us -> 0 us
  Pallas kernels: 0 us -> 142 us
  starting transfers between devices: 28.6 us -> 0 us
  matrix products: 20.5 us -> 0 us
  between operations: 14.6 us -> 0.66 us
  other arithmetic: 10.8 us -> 1.48 us
  local copies, waits for them, and re-layouts: 12.5 us -> 5.71 us
    reduce_scatter x1 -> x0, waiting for transfers between devices: 276 us -> none  [in_one_piece(): lax.psum_scatter(both, axis, scatter_dimension=dim, tiled=True)]
    unnamed x1 -> x0, blocking collectives: 176 us -> none
    pallas_call x0 -> x1, Pallas kernels: none -> 142 us  [per_device(): pl.pallas_call(kernel, name='step', out_shape=(jax.ShapeDtypeStruct((ROWS...]
    all_to_all x1 -> x0, starting transfers between devices: 28.5 us -> none  [sum_at_owner(): lax.all_to_all(tiles, axis, split_axis=0, concat_axis=0, tiled=True)]
    all_to_all x1 -> x0, waiting for transfers between devices: 24.6 us -> none  [sum_at_owner(): lax.all_to_all(tiles, axis, split_axis=0, concat_axis=0, tiled=True)]
    dot_general x5 -> x0, matrix products: 20.5 us -> none  [the longest x1 4.68 us: per_device(): lax.dot_general(codes_again, error, (((0,), (0,)), ((), ())), preferred_e...]
    all_gather x2 -> x0, blocking collectives: 14.6 us -> none  [gather_in_order(): tiles = lax.all_gather(tiles, axes[k], axis=0, tiled=True)]
  transfers between devices with their start and end apart: 6 -> 0, of which waited for: 3 -> 0; matrix products, arithmetic and copies ran while one was open for 6% -> 0% of each run, Pallas kernels for 0% -> 0%
where the time goes in v1:
time: 150 us
  Pallas kernels  142 us (95%)
  local copies, waits for them, and re-layouts  5.71 us (4%)
    pallas_call x1, Pallas kernels, per_device(): pl.pallas_call(kernel, name='step', out_shape=(jax.ShapeDtypeStruct((ROWS...  142 us
    unnamed x7, local copies, waits for them, and re-layouts  3.62 us

profile of v1, /device:TPU:1, one launch (start us, length us, event | category | flops | bytes accessed | tf_op | source)
XLA Modules:
  0.0 149.6 jit_solution(10958762720485612832)
XLA Ops:
  0.6 0.7 broadcast_in_dim.10
  1.4 1.5 pad_maximum_fusion.encb
  2.8 141.8 %step.1 = (bf16[256,2048]{1,0:T(8,128)(2,1)}, f32[16,2048]{1,0:T(8,128)}, f32[16,2048]{1,0:T(8,128)}, f32[16,128]{1,0:T(8,128)}) custom-call(f32[256,2048]{1,0:T(8,128)} %acts.1, f32[1,2048]{1,0:T(1,128)} %bitcast.1, bf16[16,2176]{1,0:T(8,128)(2,1)} %pad_maximum_fusion.encb, bf16[16,2048]{1,0:T(8,128)(2,1)} %dec.1), custom_call_target="tpu_custom_call" | custom-call | tf_op jit(solution)/shard_map/step/pallas_call | solution.py:384
  144.6 0.0 copy-start.1
  144.6 0.0 copy-start
  144.7 1.4 slice_reduce_fusion
  146.0 2.3 %copy.12 = bf16[256,2048]{1,0:T(8,128)(2,1)} copy(bf16[256,2048]{1,0:T(8,128)(2,1)} %get-tuple-element.16) | data formatting | bytes 2097152
  148.3 0.0 copy-done.1
  148.3 0.7 copy.13
  149.0 0.0 copy-done
  149.0 0.7 copy.14
Async XLA Ops:
  144.6 3.7 %copy-start.1 = (f32[16,2048]{1,0:T(8,128)S(1)}, f32[16,2048]{1,0:T(8,128)}, u32[]{:S(2)}) copy-start(f32[16,2048]{1,0:T(8,128)} %get-tuple-element.17) | copy-start | bytes 393220
  144.6 4.3 %copy-start = (f32[16,2048]{1,0:T(8,128)S(1)}, f32[16,2048]{1,0:T(8,128)}, u32[]{:S(2)}) copy-start(f32[16,2048]{1,0:T(8,128)} %get-tuple-element.18) | copy-start | bytes 393220

commit v2 on v1

--- a/solution.py
+++ b/solution.py
@@ -33,7 +33,7 @@
 
 
 def kernel(
-    acts, dbias, encb, dec, recon, genc, gdec, gbias,
+    acts, dbias, enc, bias, dec, recon, genc, gdec, gbias,
     cent, wenc, wdec, codes, codes_t, pown, psend, precv, psum, rsp, rsm, err, acc_e, acc_d, gb, cs,
     pay_e, pay_d, e_far, e_near, tot_e, e_last, d_far, d_near, tot_d, d_last, rec, ssem, rsem,
 ):
@@ -81,64 +81,59 @@
         pl.semaphore_signal(barrier, inc=1, device_id=f, device_id_type=MESH)
     pl.semaphore_wait(barrier, len(friends))
 
+    eye = lax.broadcasted_iota(jnp.int32, (OWN, OWN), 0) == lax.broadcasted_iota(jnp.int32, (OWN, OWN), 1)
+    column = jnp.sum(jnp.where(eye, bias[...].astype(F32), 0.0), axis=1, keepdims=True)
+    wenc[y, x, :, :D] = enc[...]
+    wenc[y, x, :, D:] = jnp.broadcast_to(column, (OWN, 128)).astype(BF16)
+    wdec[y, x] = dec[...]
     for d in (1, 2, 3):
-        send(encb, wenc.at[y, x], sems("we1", d), at_x(d))
+        send(wenc.at[y, x], wenc.at[y, x], sems("we1", d), at_x(d))
         send(dec, wdec.at[y, x], sems("wd1", d), at_y(d))
 
     for q in range(2):
         cent[2 * h + q] = (acts[q * PORTION : (q + 1) * PORTION] - dbias[...]).astype(BF16)
-    up = [wrap(2 * h + o, NZ) for o in (-2, -1, -4)]
-    down = [wrap(2 * h + o, NZ) for o in (3, 2, 5)]
-    for j in range(3):
-        for k in range(2):
-            sems("ap", j, k), sems("am", j, k)
+    def mirrored(even, odd):
+        return wrap(2 * h + even + zl * (odd - even), NZ)
+
+    coming = {
+        "a": [mirrored(-2, 3), mirrored(-1, 2), mirrored(-4, 5)],
+        "b": [mirrored(3, -2), mirrored(2, -1), mirrored(5, -4)],
+    }
+    outer = at_z(2 * zl - 1)
 
     def piece(p, k):
         return rows(cent, p, k)
 
     for j in range(2):
         for k in range(2):
-            @pl.when(zl == 1)
-            def _(j=j, k=k):
-                copy(piece(2 * h + j, k), piece(2 * h + j, k), sems("ap", j, k), at_z(1)).start()
-
-            @pl.when(zl == 0)
-            def _(j=j, k=k):
-                copy(piece(2 * h + 1 - j, k), piece(2 * h + 1 - j, k), sems("am", j, k), at_z(-1)).start()
-
-    wenc[y, x] = encb[...]
-    wdec[y, x] = dec[...]
-
-    def relay_acts(j, k):
-        for name, at, dz, first in (("ap", up, 1, 0), ("am", down, -1, 1)):
-            part = piece(at[j], k)
-            arrive(part, sems(name, j, k))
-
-            @pl.when(zl == first)
-            def _():
-                copy(part, part, sems(name, j, k), at_z(dz)).start()
-
-            if j == 0:
-                @pl.when(zl != first)
-                def _():
-                    copy(part, part, sems(name, 2, k), at_z(dz)).start()
-
-            send(part, part, sems(name + "c", j, k), partner)
-
-    def from_partner(j):
-        for name, at in (("ap", up), ("am", down)):
+            part = piece(mirrored(1 - j, j), k)
+            send(part, part, sems("a", j, k), outer)
+
+    def relay_acts(name, j, k):
+        part = piece(coming[name][j], k)
+        arrive(part, sems(name, j, k))
+        if name == "a":
+            send(part, part, sems("b", j, k), pair)
+        elif j == 0:
+            send(part, part, sems("a", 2, k), outer)
+        send(part, part, sems(name + "c", j, k), partner)
+
+    def from_partner(name, js):
+        for j in js:
             for k in range(2):
-                arrive(rows(cent, at[j], k, 1 - c), sems(name + "c", j, k))
-
-    relay_acts(0, 0)
+                arrive(rows(cent, coming[name][j], k, 1 - c), sems(name + "c", j, k))
+
+    relay_acts("a", 0, 0)
     for d in (1, 2, 3):
         arrive(wenc.at[y, wrap(x - d, SIDE)], sems("we1", d))
         arrive(wdec.at[wrap(y - d, SIDE), x], sems("wd1", d))
     for s in (1, -1):
         send(wenc.at[y], wenc.at[y], sems("we2", s), at_y(s))
         send(wdec.at[:, x], wdec.at[:, x], sems("wd2", s), at_x(s))
-    relay_acts(0, 1)
-    relay_acts(1, 0)
+    relay_acts("a", 0, 1)
+    relay_acts("b", 0, 0)
+    relay_acts("a", 1, 0)
+    relay_acts("b", 0, 1)
     for s in (1, -1):
         half = pl.ds(0 if s == 1 else 2, 2)
         yn, xn = wrap(y - s, SIDE), wrap(x - s, SIDE)
@@ -146,8 +141,9 @@
         send(wenc.at[yn, half], wenc.at[yn, half], sems("we3", s), at_y(s))
         arrive(wdec.at[:, xn], sems("wd2", s))
         send(wdec.at[half, xn], wdec.at[half, xn], sems("wd3", s), at_x(s))
-    relay_acts(1, 1)
-    relay_acts(2, 0)
+    relay_acts("a", 1, 1)
+    relay_acts("b", 1, 0)
+    relay_acts("a", 2, 0)
     for s in (1, -1):
         half = pl.ds(0 if s == 1 else 2, 2)
         arrive(wenc.at[wrap(y + 2, SIDE), half], sems("we3", s))
@@ -179,15 +175,20 @@
 
     near = 1 - 2 * zl
     blocks = [h, wrap(h - near, SIDE), wrap(h + near, SIDE), wrap(h + 2, SIDE)]
+    relay_acts("b", 1, 1)
     cs[...] = encode(blocks[0])
-    relay_acts(2, 1)
+    relay_acts("a", 2, 1)
     decode(blocks[0], 0)
-    from_partner(0)
-    from_partner(1)
-    for i in (1, 2):
-        cs[...] += encode(blocks[i])
-        decode(blocks[i], i)
-    from_partner(2)
+    relay_acts("b", 2, 0)
+    from_partner("a", (0, 1))
+    cs[...] += encode(blocks[1])
+    decode(blocks[1], 1)
+    relay_acts("b", 2, 1)
+    from_partner("b", (0, 1))
+    cs[...] += encode(blocks[2])
+    decode(blocks[2], 2)
+    from_partner("a", (2,))
+    from_partner("b", (2,))
     cs[...] += encode(blocks[3])
     decode(blocks[3], 3)
 
@@ -370,16 +371,11 @@
     total = owned(y, tot_d, d_last, "d")
     gdec[...] = scale * (total + SPARSITY * col_sums * mine / own_norms)
 
-    for name, at, dz in (("ap", up, 1), ("am", down, -1)):
-        for j in range(3):
-            for k in range(2):
-                copy(piece(at[j], k), piece(at[j], k), sems(name, j, k), at_z(dz)).wait_send()
     for cp in pending:
         cp.wait_send()
 
 
 def per_device(acts, dec_bias, enc_weight, enc_bias, dec_weight):
-    encb = jnp.concatenate([enc_weight, jnp.broadcast_to(enc_bias[:, None], (OWN, 128))], axis=1)
     vmem = pl.BlockSpec(memory_space=pltpu.VMEM)
     recon, genc, gdec, gbias = pl.pallas_call(
         kernel,
@@ -390,7 +386,7 @@
             jax.ShapeDtypeStruct((OWN, D), F32),
             jax.ShapeDtypeStruct((OWN, 128), F32),
         ),
-        in_specs=[vmem] * 4,
+        in_specs=[vmem] * 5,
         out_specs=(vmem,) * 4,
         scratch_shapes=[
             pltpu.VMEM((NZ, PORTION, D), BF16),
@@ -424,7 +420,7 @@
             pltpu.SemaphoreType.DMA((N_SEMS,)),
         ],
         compiler_params=pltpu.CompilerParams(collective_id=0, has_side_effects=True, vmem_limit_bytes=60 << 20),
-    )(acts, dec_bias[None, :], encb, dec_weight)
+    )(acts, dec_bias[None, :], enc_weight, enc_bias[None, :], dec_weight)
     return recon, genc, gdec, gbias[:, 0]
 
 

time: 150 us -> 115 us (0.77)
  Pallas kernels: 142 us -> 109 us
    pallas_call x1, Pallas kernels: 142 us -> 109 us  [per_device(): pl.pallas_call(kernel, name='step', out_shape=(jax.ShapeDtypeStruct((ROWS...]
where the time goes in v2:
time: 115 us
  Pallas kernels  109 us (95%)
  local copies, waits for them, and re-layouts  4.99 us (4%)
    pallas_call x1, Pallas kernels, per_device(): pl.pallas_call(kernel, name='step', out_shape=(jax.ShapeDtypeStruct((ROWS...  109 us
    unnamed x7, local copies, waits for them, and re-layouts  3.62 us

profile of v2, /device:TPU:1, one launch (start us, length us, event | category | flops | bytes accessed | tf_op | source)
XLA Modules:
  0.0 115.0 jit_solution(14122649249806566977)
XLA Ops:
  0.6 109.4 %step.1 = (bf16[256,2048]{1,0:T(8,128)(2,1)}, f32[16,2048]{1,0:T(8,128)}, f32[16,2048]{1,0:T(8,128)}, f32[16,128]{1,0:T(8,128)}) custom-call(f32[256,2048]{1,0:T(8,128)} %acts.1, f32[1,2048]{1,0:T(1,128)} %bitcast.2, bf16[16,2048]{1,0:T(8,128)(2,1)} %enc.1, bf16[1,16]{1,0:T(2,128)(2,1)} %bitcast.3, bf16[16,2048]{1,0:T(8,128)(2,1)} %dec.1), custom_call_target="tpu_custom_call" | custom-call | tf_op jit(solution)/shard_map/step/pallas_call | solution.py:380
  110.0 0.0 copy-start.1
  110.0 0.0 copy-start
  110.0 1.4 %slice_reduce_fusion = f32[16]{0:T(128)} fusion(f32[16,128]{1,0:T(8,128)} %get-tuple-element.11), kind=kLoop, calls=%fused_computation | loop fusion | bytes 128 | tf_op jit(solution)/shard_map/slice | solution.py:424
  111.4 2.3 %copy.12 = bf16[256,2048]{1,0:T(8,128)(2,1)} copy(bf16[256,2048]{1,0:T(8,128)(2,1)} %get-tuple-element.16) | data formatting | bytes 2097152
  113.7 0.0 copy-done.1
  113.7 0.7 copy.13
  114.4 0.0 copy-done
  114.4 0.7 copy.14
Async XLA Ops:
  110.0 3.7 %copy-start.1 = (f32[16,2048]{1,0:T(8,128)S(1)}, f32[16,2048]{1,0:T(8,128)}, u32[]{:S(2)}) copy-start(f32[16,2048]{1,0:T(8,128)} %get-tuple-element.17) | copy-start | bytes 393220
  110.0 4.3 %copy-start = (f32[16,2048]{1,0:T(8,128)S(1)}, f32[16,2048]{1,0:T(8,128)}, u32[]{:S(2)}) copy-start(f32[16,2048]{1,0:T(8,128)} %get-tuple-element.18) | copy-start | bytes 393220

commit v3 on v2

--- a/solution.py
+++ b/solution.py
@@ -33,9 +33,9 @@
 
 
 def kernel(
-    acts, dbias, enc, bias, dec, recon, genc, gdec, gbias,
+    acts_hbm, dbias_hbm, enc_hbm, bias_hbm, dec_hbm, recon, genc, gdec, gbias, acts, dbias, bias, dec,
     cent, wenc, wdec, codes, codes_t, pown, psend, precv, psum, rsp, rsm, err, acc_e, acc_d, gb, cs,
-    pay_e, pay_d, e_far, e_near, tot_e, e_last, d_far, d_near, tot_d, d_last, rec, ssem, rsem,
+    pay_e, pay_d, e_far, e_near, tot_e, e_last, d_far, d_near, tot_d, d_last, rec, lsem, ssem, rsem,
 ):
     zl, c, y, x, h = [lax.axis_index(a) for a in AXES]
     z = 2 * h + zl
@@ -75,23 +75,38 @@
         who = c if core is None else core
         return ref.at[p, pl.ds(pl.multiple_of(who * SUB + k * CH, CH), CH)]
 
+    loads = [
+        pltpu.make_async_copy(src, dst, lsem.at[i])
+        for i, (src, dst) in enumerate(
+            (
+                (bias_hbm, bias),
+                (enc_hbm, wenc.at[y, x, :, pl.ds(0, D)]),
+                (dec_hbm, dec),
+                (dbias_hbm, dbias),
+                (acts_hbm, acts),
+            )
+        )
+    ]
+    for load in loads:
+        load.start()
     barrier = pltpu.get_barrier_semaphore()
     friends = [partner, at_z(1), at_z(-1)] + [at_y(d) for d in (1, 2, 3)] + [at_x(d) for d in (1, 2, 3)]
     for f in friends:
         pl.semaphore_signal(barrier, inc=1, device_id=f, device_id_type=MESH)
-    pl.semaphore_wait(barrier, len(friends))
-
+    for load in loads:
+        load.wait()
+    for q in range(2):
+        cent[2 * h + q] = (acts[q * PORTION : (q + 1) * PORTION] - dbias[...]).astype(BF16)
     eye = lax.broadcasted_iota(jnp.int32, (OWN, OWN), 0) == lax.broadcasted_iota(jnp.int32, (OWN, OWN), 1)
     column = jnp.sum(jnp.where(eye, bias[...].astype(F32), 0.0), axis=1, keepdims=True)
-    wenc[y, x, :, :D] = enc[...]
     wenc[y, x, :, D:] = jnp.broadcast_to(column, (OWN, 128)).astype(BF16)
     wdec[y, x] = dec[...]
+    pl.semaphore_wait(barrier, len(friends))
+
     for d in (1, 2, 3):
         send(wenc.at[y, x], wenc.at[y, x], sems("we1", d), at_x(d))
         send(dec, wdec.at[y, x], sems("wd1", d), at_y(d))
 
-    for q in range(2):
-        cent[2 * h + q] = (acts[q * PORTION : (q + 1) * PORTION] - dbias[...]).astype(BF16)
     def mirrored(even, odd):
         return wrap(2 * h + even + zl * (odd - even), NZ)
 
@@ -364,7 +379,8 @@
     scale = (ROWS * SIDE * SIDE * SIDE) ** -0.5
     total = owned(x, tot_e, e_last, "e")
     genc[...] = scale * total[:, :D]
-    gbias[...] = jnp.broadcast_to(scale * jnp.sum(total[:, D : D + 128], axis=1, keepdims=True), (OWN, 128))
+    bias_sums = scale * jnp.sum(total[:, D : D + 128], axis=1, keepdims=True)
+    gbias[...] = jnp.sum(jnp.where(eye, bias_sums, 0.0), axis=0, keepdims=True)
     col_sums = jnp.sum(total[:, D + 128 :], axis=1, keepdims=True)
     mine = dec[...].astype(F32)
     own_norms = jnp.sqrt(jnp.sum(mine * mine, axis=1, keepdims=True) + 1e-06)
@@ -375,20 +391,29 @@
         cp.wait_send()
 
 
+def store(*refs):
+    sources, results, sem = refs[:4], refs[4:8], refs[8]
+    copies = [pltpu.make_async_copy(a, b, sem.at[i]) for i, (a, b) in enumerate(zip(sources, results))]
+    for cp in copies:
+        cp.start()
+    for cp in copies:
+        cp.wait()
+
+
 def per_device(acts, dec_bias, enc_weight, enc_bias, dec_weight):
-    vmem = pl.BlockSpec(memory_space=pltpu.VMEM)
-    recon, genc, gdec, gbias = pl.pallas_call(
+    vmem, anywhere = pl.BlockSpec(memory_space=pltpu.VMEM), pl.BlockSpec(memory_space=pl.ANY)
+    results = (((ROWS, D), BF16), ((OWN, D), F32), ((OWN, D), F32), ((1, OWN), F32))
+    in_vmem = pl.pallas_call(
         kernel,
         name="step",
-        out_shape=(
-            jax.ShapeDtypeStruct((ROWS, D), BF16),
-            jax.ShapeDtypeStruct((OWN, D), F32),
-            jax.ShapeDtypeStruct((OWN, D), F32),
-            jax.ShapeDtypeStruct((OWN, 128), F32),
-        ),
-        in_specs=[vmem] * 5,
+        out_shape=tuple(pltpu.VMEM(*r) for r in results),
+        in_specs=[anywhere] * 5,
         out_specs=(vmem,) * 4,
         scratch_shapes=[
+            pltpu.VMEM((ROWS, D), F32),
+            pltpu.VMEM((1, D), F32),
+            pltpu.VMEM((1, OWN), BF16),
+            pltpu.VMEM((OWN, D), BF16),
             pltpu.VMEM((NZ, PORTION, D), BF16),
             pltpu.VMEM((SIDE, SIDE, OWN, WE), BF16),
             pltpu.VMEM((SIDE, SIDE, OWN, D), BF16),
@@ -416,12 +441,21 @@
             pltpu.VMEM((SIDE, OWN, D), BF16),
             pltpu.VMEM((3, OWN, D), BF16),
             pltpu.VMEM((ROWS, D), BF16),
+            pltpu.SemaphoreType.DMA((5,)),
             pltpu.SemaphoreType.DMA((N_SEMS,)),
             pltpu.SemaphoreType.DMA((N_SEMS,)),
         ],
         compiler_params=pltpu.CompilerParams(collective_id=0, has_side_effects=True, vmem_limit_bytes=60 << 20),
     )(acts, dec_bias[None, :], enc_weight, enc_bias[None, :], dec_weight)
-    return recon, genc, gdec, gbias[:, 0]
+    recon, genc, gdec, gbias = pl.pallas_call(
+        store,
+        name="store",
+        out_shape=tuple(jax.ShapeDtypeStruct(*r) for r in results),
+        in_specs=[vmem] * 4,
+        out_specs=(anywhere,) * 4,
+        scratch_shapes=[pltpu.SemaphoreType.DMA((4,))],
+    )(*[pltpu.with_memory_space_constraint(r, pltpu.VMEM) for r in in_vmem])
+    return recon, genc, gdec, gbias[0]
 
 
 def solution(mesh):

time: 115 us -> 108 us (0.939)
  local copies, waits for them, and re-layouts: 4.99 us -> 0 us
    unnamed x7 -> x0, local copies, waits for them, and re-layouts: 3.62 us -> none
    pallas_call x1 -> x2, Pallas kernels: 109 us -> 108 us  [the longest x1 106 us: per_device(): pl.pallas_call(kernel, name='step', out_shape=tuple((pltpu.VMEM(*r) for r...]
    slice x1 -> x0, local copies, waits for them, and re-layouts: 1.36 us -> none  [per_device(): return (recon, genc, gdec, gbias[:, 0])]
where the time goes in v3:
time: 108 us
  Pallas kernels  108 us (100%)
    pallas_call x1, Pallas kernels, per_device(): pl.pallas_call(kernel, name='step', out_shape=tuple((pltpu.VMEM(*r) for r...  106 us

profile of v3, /device:TPU:1, one launch (start us, length us, event | category | flops | bytes accessed | tf_op | source)
XLA Modules:
  0.0 108.2 jit_solution(17334761774349235887)
XLA Ops:
  0.6 106.5 %step.1 = (bf16[256,2048]{1,0:T(8,128)(2,1)S(1)}, f32[16,2048]{1,0:T(8,128)S(1)}, f32[16,2048]{1,0:T(8,128)S(1)}, f32[1,16]{1,0:T(1,128)S(1)}) custom-call(f32[256,2048]{1,0:T(8,128)} %acts_hbm.1, f32[1,2048]{1,0:T(1,128)} %bitcast.3, bf16[16,2048]{1,0:T(8,128)(2,1)} %enc_hbm.1, bf16[1,16]{1,0:T(2,128)(2,1)} %bitcast.4, bf16[16,2048]{1,0:T(8,128)(2,1)} %dec_hbm.1), custom_call_target="tpu_custom_call" | custom-call | tf_op jit(solution)/shard_map/step/pallas_call | solution.py:406
  107.1 1.1 %store.1 = (bf16[256,2048]{1,0:T(8,128)(2,1)}, f32[16,2048]{1,0:T(8,128)}, f32[16,2048]{1,0:T(8,128)}, f32[1,16]{1,0:T(1,128)}) custom-call(bf16[256,2048]{1,0:T(8,128)(2,1)S(1)} %get-tuple-element.12.refs_0_, f32[16,2048]{1,0:T(8,128)S(1)} %get-tuple-element.13.refs_1_, f32[16,2048]{1,0:T(8,128)S(1)} %get-tuple-element.14.refs_2_, ...), custom_call_target="tpu_custom_call" | custom-call | tf_op jit(solution)/shard_map/store/pallas_call | solution.py:450

commit v4 on v3

v4 whole, which is shorter than its diff:
```python
import jax
import jax.numpy as jnp
from jax import lax
from jax.experimental import pallas as pl
from jax.experimental.pallas import tpu as pltpu
from jax.sharding import Mesh
from jax.sharding import PartitionSpec as P


AXES = ("zl", "c", "y", "x", "h")
MESH = pl.DeviceIdType.MESH
F32, BF16 = jnp.float32, jnp.bfloat16
SPARSITY = 0.5
NZ, SIDE, ROWS, D, OWN, LAT = 8, 4, 256, 2048, 16, 256
PORTION = ROWS // 2
SUB = PORTION // 2
CH = SUB // 2
STRIP = CH // 2
WE = D + 128
STATS = 256
GE = STATS + D
TILE = 512


class Semaphores:
    def __init__(self):
        self.names = {}

    def __call__(self, *name):
        return self.names.setdefault(name, len(self.names))


N_ARRIVE, N_LEAVE = 104, 18
NT = (((1,), (1,)), ((), ()))


def kernel(
    acts_hbm, dbias_hbm, enc_hbm, bias_hbm, dec_hbm, recon, genc, gdec, gbias, acts, dbias, bias, dec,
    cent, wenc, wdec, codes, codes_t, pown, psend, precv, psum, rsp, rsm, err, acc_e, acc_d, gb, cs,
    pay_e, pay_d, e_far, e_near, tot_e, e_last, d_far, d_near, tot_d, d_last, rec, lsem, ssem, rsem,
):
    zl, c, y, x, h = [lax.axis_index(a) for a in AXES]
    z = 2 * h + zl
    sems, kinds = Semaphores(), Semaphores()

    def wrap(v, n):
        return lax.rem(v + 2 * n, n)

    def at_z(dz):
        q = wrap(z + dz, NZ)
        return (lax.rem(q, 2), c, y, x, lax.div(q, 2))

    def at_y(dy):
        return (zl, c, wrap(y + dy, SIDE), x, h)

    def at_x(dx):
        return (zl, c, y, wrap(x + dx, SIDE), h)

    partner = (zl, 1 - c, y, x, h)
    pair = (1 - zl, c, y, x, h)

    def copy(src, dst, dev, leaves, arrives):
        return pltpu.make_async_remote_copy(
            src_ref=src, dst_ref=dst, send_sem=ssem.at[leaves], recv_sem=rsem.at[arrives], device_id=dev, device_id_type=MESH
        )

    def send(src, dst, arrives, dev, kind):
        copy(src, dst, dev, kinds(kind), arrives).start()

    def arrive(dst, sem):
        copy(dst, dst, partner, 0, sem).wait_recv()

    def left(src, kind):
        copy(src, src, partner, kinds(kind), 0).wait_send()

    def rows(ref, p, k, core=None):
        return ref.at[k, p, c if core is None else core]

    loads = [
        pltpu.make_async_copy(src, dst, lsem.at[i])
        for i, (src, dst) in enumerate(
            (
                (bias_hbm, bias),
                (enc_hbm, wenc.at[y, x, :, pl.ds(0, D)]),
                (dec_hbm, dec),
                (dbias_hbm, dbias),
                (acts_hbm, acts),
            )
        )
    ]
    for load in loads:
        load.start()
    barrier = pltpu.get_barrier_semaphore()
    friends = [partner, at_z(1), at_z(-1)] + [at_y(d) for d in (1, 2, 3)] + [at_x(d) for d in (1, 2, 3)]
    for f in friends:
        pl.semaphore_signal(barrier, inc=1, device_id=f, device_id_type=MESH)
    for load in loads:
        load.wait()
    for q in range(2):
        for who in range(2):
            for k in range(2):
                at = q * PORTION + who * SUB + k * CH
                cent[k, 2 * h + q, who] = (acts[at : at + CH] - dbias[...]).astype(BF16)
    eye = lax.broadcasted_iota(jnp.int32, (OWN, OWN), 0) == lax.broadcasted_iota(jnp.int32, (OWN, OWN), 1)
    column = jnp.sum(jnp.where(eye, bias[...].astype(F32), 0.0), axis=1, keepdims=True)
    wenc[y, x, :, D:] = jnp.broadcast_to(column, (OWN, 128)).astype(BF16)
    wdec[y, x] = dec[...]
    pl.semaphore_wait(barrier, len(friends))

    for d in (1, 2, 3):
        send(wenc.at[y, x], wenc.at[y, x], sems("we1"), at_x(d), "we1")
        send(dec, wdec.at[y, x], sems("wd1"), at_y(d), "wd1")

    def mirrored(even, odd):
        return wrap(2 * h + even + zl * (odd - even), NZ)

    coming = {
        "a": [mirrored(-2, 3), mirrored(-1, 2), mirrored(-4, 5)],
        "b": [mirrored(3, -2), mirrored(2, -1), mirrored(5, -4)],
    }
    outer = at_z(2 * zl - 1)

    def piece(p, k):
        return rows(cent, p, k)

    def send_own(j, k):
        part = piece(mirrored(1 - j, j), k)
        send(part, part, sems("a", j, k), outer, "acts")

    send_own(0, 0)
    send_own(1, 0)
    send_own(0, 1)

    def relay_acts(name, j, k):
        part = piece(coming[name][j], k)
        arrive(part, sems(name, j, k))
        if name == "a":
            send(part, part, sems("b", j, k), pair, "acts")
        elif j == 0:
            send(part, part, sems("a", 2, k), outer, "acts")
        send(part, part, sems("early" if name == "a" and j < 2 else "late", k), partner, "acts")

    def from_partner(which, k):
        arrive(cent.at[0, pl.ds(0, 1 if which == "early" else 2)], sems(which, k))

    relay_acts("a", 0, 0)
    arrive(wenc.at[0, pl.ds(0, 3)], sems("we1"))
    arrive(wdec.at[0, pl.ds(0, 3)], sems("wd1"))
    for i in range(2):
        for s in (1, -1):
            half = pl.ds(0 if (s == 1) == (i == 0) else 2, 2)
            order = s if i == 0 else 0
            send(wenc.at[y, half], wenc.at[y, half], sems("we2", order), at_y(s), "we2")
            send(wdec.at[half, x], wdec.at[half, x], sems("wd2", order), at_x(s), "wd2")
    relay_acts("a", 1, 0)
    relay_acts("b", 0, 0)
    send_own(1, 1)
    relay_acts("a", 0, 1)
    relay_acts("b", 1, 0)
    for s in (1, -1):
        half = pl.ds(0 if s == 1 else 2, 2)
        yn, xn = wrap(y - s, SIDE), wrap(x - s, SIDE)
        arrive(wenc.at[yn, half], sems("we2", s))
        send(wenc.at[yn, half], wenc.at[yn, half], sems("we2", 0), at_y(s), "we2")
        arrive(wdec.at[half, xn], sems("wd2", s))
        send(wdec.at[half, xn], wdec.at[half, xn], sems("wd2", 0), at_x(s), "wd2")
    relay_acts("a", 2, 0)
    relay_acts("b", 0, 1)
    relay_acts("a", 1, 1)
    arrive(wenc.at[pl.ds(0, 2)], sems("we2", 0))
    arrive(wdec.at[pl.ds(0, 2)], sems("wd2", 0))

    def encode(k, pair_of):
        block = jnp.concatenate([cent[k, pl.ds(2 * b, 2)].reshape(PORTION, D) for b in pair_of], axis=0)
        weights = wenc[:, :, :, :D].reshape(LAT, D)
        shift = wenc[:, :, :, D:].reshape(LAT, 128).astype(F32)
        pre = lax.dot_general(weights, block, NT, preferred_element_type=F32)
        value = jnp.maximum(pre + jnp.concatenate([shift, shift], axis=1), 0.0)
        turned = value.T.astype(BF16)
        for i, b in enumerate(pair_of):
            for q in range(2):
                for who in range(2):
                    at = i * PORTION + q * SUB + who * CH
                    codes[k, b, who, q * CH : (q + 1) * CH] = turned[at : at + CH]
            codes_t[k, b] = value[:, i * PORTION : (i + 1) * PORTION].astype(BF16)
        folded = value[:, :128] + value[:, 128:]
        cs[...] = folded if k == 0 and pair_of is early else cs[...] + folded

    def decode(k, pair_of):
        left = [jnp.concatenate([codes[k, b, who] for b in pair_of], axis=0) for who in (1 - c, c)]
        for t in range(0, D, TILE):
            right = wdec[:, :, :, t : t + TILE].reshape(LAT, TILE)
            other = jnp.dot(left[0], right, preferred_element_type=F32).astype(BF16)
            mine = jnp.dot(left[1], right, preferred_element_type=F32)
            for i, b in enumerate(pair_of):
                for q in range(2):
                    r = slice((2 * i + q) * CH, (2 * i + q + 1) * CH)
                    psend[k, 2 * b + q, :, t : t + TILE] = other[r]
                    pown[k, 2 * b + q, :, t : t + TILE] = mine[r]
        for i, b in enumerate(pair_of):
            for q in range(2):
                part = precv.at[k, 2 * b + q]
                send(psend.at[k, 2 * b + q], part, sems("px", k), partner, "px")

    def decoded(k):
        arrive(precv.at[k], sems("px", k))

    def strip(r):
        return pl.ds(r * STRIP, STRIP)

    def farthest(sign, r):
        return (sign == 1) == (r == 0)

    def part_sum(k, p, r):
        return pown[k, p, strip(r)] + precv[k, p, strip(r)].astype(F32)

    def pass_on(sign, k, r, away):
        buf, name = (rsp, "rp") if sign == 1 else (rsm, "rm")
        p = wrap(z + sign * away, NZ)
        part = psum.at[k, p, strip(r)]
        total = part_sum(k, p, r)
        if away < (4 if farthest(sign, r) else 3):
            arrive(buf.at[k, away, strip(r)], sems(name, k, r, away + 1))
            total = total + buf[k, away, strip(r)].astype(F32)
        part[...] = total.astype(BF16)
        send(part, buf.at[k, away - 1, strip(r)], sems(name, k, r, away), at_z(sign), "sums")

    def steps(k, *which):
        for n in which:
            r, away = ((0, 4), (1, 3), (0, 3), (1, 2), (0, 2), (1, 1), (0, 1))[n - 1]
            pass_on(1, k, r, away)
            pass_on(-1, k, 1 - r, away)

    near = 1 - 2 * zl
    blocks = [h, wrap(h - near, SIDE), wrap(h + near, SIDE), wrap(h + 2, SIDE)]
    early, late = tuple(blocks[:2]), tuple(blocks[2:])
    relay_acts("b", 2, 0)
    from_partner("early", 0)
    encode(0, early)
    relay_acts("a", 2, 1)
    decode(0, early)
    from_partner("late", 0)
    encode(0, late)
    decode(0, late)
    relay_acts("b", 1, 1)
    from_partner("early", 1)
    encode(1, early)
    decoded(0)
    steps(0, 1, 2)
    decode(1, early)
    relay_acts("b", 2, 1)
    from_partner("late", 1)
    encode(1, late)
    decode(1, late)
    steps(0, 3, 4)
    decoded(1)
    for n, m in ((1, 5), (2, 6)):
        steps(1, n)
        steps(0, m)
    steps(0, 7)
    steps(1, 3, 4)

    own_rows = zl * PORTION + c * SUB

    def at_home(k):
        for r in range(2):
            at = k * CH + r * STRIP
            here = pl.ds(pl.multiple_of(own_rows + at, STRIP), STRIP)
            total = part_sum(k, z, r) + dbias[...]
            arrive(rsp.at[k, 0, strip(r)], sems("rp", k, r, 1))
            arrive(rsm.at[k, 0, strip(r)], sems("rm", k, r, 1))
            full = total + rsp[k, 0, strip(r)].astype(F32) + rsm[k, 0, strip(r)].astype(F32)
            rec[here] = full.astype(BF16)
            err[k, z, c, strip(r)] = (full - acts[here]).astype(BF16)
            mine = rows(err, z, k).at[strip(r)]
            send(mine, mine, sems("gp", 0, k, r), at_z(1), "err")
            send(mine, mine, sems("gm", 0, k, r), at_z(-1), "err")
            send(mine, mine, sems("errc", 0), partner, "errc")

    at_home(0)
    steps(1, 5, 6, 7)

    norms = []
    for q in range(2):
        rows_q = wdec[2 * q : 2 * q + 2].reshape(LAT // 2, D).astype(F32)
        norms.append(jnp.sqrt(jnp.sum(rows_q * rows_q, axis=1, keepdims=True) + 1e-06))
    norms = jnp.concatenate(norms, axis=0)

    def incoming(s, k, r, sign, core=None):
        return rows(err, wrap(z - sign * (s + 1), NZ), k, core).at[strip(r)]

    def relay_err(s, k):
        for r in range(2):
            for sign, name in ((1, "gp"), (-1, "gm")):
                if s == 3 and not farthest(sign, r):
                    continue
                part = incoming(s, k, r, sign)
                arrive(part, sems(name, s, k, r))
                if s < 2 or (s == 2 and farthest(sign, r)):
                    send(part, part, sems(name, s + 1, k, r), at_z(sign), "err")
                send(part, part, sems("errc", s), partner, "errc")

    def err_from_partner(s):
        arrive(err.at[0, pl.ds(0, (3, 2, 2, 1)[s])], sems("errc", s))

    def backward(b, first, last):
        block = err[:, pl.ds(2 * b, 2)].reshape(ROWS, D)
        weights = wdec[...].reshape(LAT, D)
        back = lax.dot_general(weights, block, NT, preferred_element_type=F32)
        kept = jnp.concatenate([codes_t[0, b], codes_t[1, b]], axis=1)
        grad_pre = jnp.where(kept.astype(F32) > 0.0, back + SPARSITY * norms, 0.0)
        folded = grad_pre[:, :128] + grad_pre[:, 128:]
        gb[...] = folded if first else gb[...] + folded
        grad_bf = grad_pre.astype(BF16)
        if last:
            pay_e[:, :, :, :128] = gb[...].astype(BF16).reshape(SIDE, SIDE, OWN, 128)
            pay_e[:, :, :, 128:STATS] = cs[...].astype(BF16).reshape(SIDE, SIDE, OWN, 128)
        for left, data, acc, pay in ((grad_bf, cent, acc_e, pay_e), (kept, err, acc_d, pay_d)):
            for t in range(0, D, TILE):
                right = data[:, pl.ds(2 * b, 2), :, :, t : t + TILE].reshape(ROWS, TILE)
                total = jnp.dot(left, right, preferred_element_type=F32)
                if not first:
                    total = total + acc[:, t : t + TILE]
                if not last:
                    acc[:, t : t + TILE] = total
                    continue
                at = t + (STATS if pay is pay_e else 0)
                pay[:, :, :, at : at + TILE] = total.astype(BF16).reshape(SIDE, SIDE, OWN, TILE)
                if t % (D // 2) == D // 2 - TILE:
                    (start_e if pay is pay_e else start_d)(2 * t // D)

    low, high = pl.ds(0, 2), pl.ds(2, 2)

    def e_part(yy, half, cols):
        return pay_e.at[yy, half, :, cols]

    def d_part(xx, half, cols):
        return pay_d.at[half, xx, :, cols]

    E_COLS = [pl.ds(0, STATS + D // 2), pl.ds(STATS + D // 2, D // 2)]
    D_COLS = [pl.ds(0, D // 2), pl.ds(D // 2, D // 2)]

    def start(i, cols, part, v, far, close, name, at):
        for n, s, summed, plain in ((0, 1, low, high), (1, -1, high, low)):
            send(part(wrap(v + 2, SIDE), summed, cols), far.at[n, :, :, cols], sems(name, "far", s, i), at(s), (name, i))
        for n, s, summed, plain in ((0, 1, low, high), (1, -1, high, low)):
            send(part(wrap(v + s, SIDE), plain, cols), close.at[n, plain, :, cols], sems(name, "near", i), at(s), (name, i))

    def start_e(i):
        start(i, E_COLS[i], e_part, y, e_far, e_near, "e", at_y)

    def start_d(i):
        start(i, D_COLS[i], d_part, x, d_far, d_near, "d", at_x)

    def forward_sum(i, cols, part, v, far, close, name, at):
        for n, s, half in ((0, 1, low), (1, -1, high)):
            arrive(far.at[n, :, :, cols], sems(name, "far", s, i))
            block = part(wrap(v + s, SIDE), half, cols)
            block[...] = (block[...].astype(F32) + far[n, :, :, cols].astype(F32)).astype(BF16)
            send(block, close.at[n, half, :, cols], sems(name, "near", i), at(s), (name, i))

    def at_owner(i, cols, part, v, w, close, tot, last, name, at):
        arrive(close.at[:, :, :, cols], sems(name, "near", i))
        tot[:, :, cols] = (
            part(v, pl.ds(0, SIDE), cols)[...].astype(F32)
            + close[0, :, :, cols].astype(F32)
            + close[1, :, :, cols].astype(F32)
        ).astype(BF16)
        for d in (2, 1, 3):
            send(tot.at[wrap(w + d, SIDE), :, cols], last.at[d - 1, :, cols], sems(name, "last", i), at(d), (name, "last", i))

    def owned(i, cols, w, tot, last, name):
        total = tot[w, :, cols].astype(F32)
        arrive(last.at[:, :, cols], sems(name, "last", i))
        for d in (1, 2, 3):
            total = total + last[d - 1, :, cols].astype(F32)
        return total

    relay_err(0, 0)
    at_home(1)
    relay_err(1, 0)
    relay_err(0, 1)
    relay_err(2, 0)
    relay_err(1, 1)
    err_from_partner(0)
    backward(blocks[0], True, False)
    relay_err(3, 0)
    err_from_partner(1)
    backward(blocks[1], False, False)
    relay_err(2, 1)
    err_from_partner(2)
    backward(blocks[2], False, False)
    relay_err(3, 1)
    own_rec = rec.at[pl.ds(pl.multiple_of(own_rows, SUB), SUB)]
    send(own_rec, own_rec, sems("rc"), partner, "rec")
    send(own_rec, own_rec, sems("rz"), pair, "rec")
    err_from_partner(3)
    backward(blocks[3], False, True)

    for i in range(2):
        forward_sum(i, E_COLS[i], e_part, y, e_far, e_near, "e", at_y)
        forward_sum(i, D_COLS[i], d_part, x, d_far, d_near, "d", at_x)
    pair_rec = rec.at[pl.ds(pl.multiple_of((1 - zl) * PORTION + c * SUB, SUB), SUB)]
    arrive(pair_rec, sems("rz"))
    send(pair_rec, pair_rec, sems("rc"), partner, "rec")
    for i in range(2):
        at_owner(i, E_COLS[i], e_part, y, x, e_near, tot_e, e_last, "e", at_x)
        at_owner(i, D_COLS[i], d_part, x, y, d_near, tot_d, d_last, "d", at_y)
    arrive(rec.at[pl.ds(0, 2 * SUB)], sems("rc"))
    recon[...] = rec[...]

    scale = (ROWS * SIDE * SIDE * SIDE) ** -0.5
    mine = dec[...].astype(F32)
    own_norms = jnp.sqrt(jnp.sum(mine * mine, axis=1, keepdims=True) + 1e-06)
    sides = [pl.ds(0, D // 2), pl.ds(D // 2, D // 2)]
    for i in range(2):
        total = owned(i, E_COLS[i], x, tot_e, e_last, "e")
        genc[:, sides[i]] = scale * (total[:, STATS:] if i == 0 else total)
        if i == 0:
            bias_sums = scale * jnp.sum(total[:, :128], axis=1, keepdims=True)
            gbias[...] = jnp.sum(jnp.where(eye, bias_sums, 0.0), axis=0, keepdims=True)
            sparse = SPARSITY * jnp.sum(total[:, 128:STATS], axis=1, keepdims=True) * mine / own_norms
        total = owned(i, D_COLS[i], y, tot_d, d_last, "d")
        gdec[:, sides[i]] = scale * (total + sparse[:, i * (D // 2) : (i + 1) * (D // 2)])

    left(wenc.at[0, pl.ds(0, 3)], "we1")
    left(wdec.at[0, pl.ds(0, 3)], "wd1")
    left(wenc.at[pl.ds(0, 3)], "we2")
    left(wdec.at[pl.ds(0, 3)], "wd2")
    left(cent.at[:, pl.ds(0, 6)], "acts")
    left(cent.at[0], "px")
    left(cent.at[0, pl.ds(0, 7)], "sums")
    left(cent.at[0, pl.ds(0, 7)], "err")
    left(cent.at[0], "errc")
    left(rec.at[pl.ds(0, 3 * SUB)], "rec")
    for i in range(2):
        left(pay_e.at[pl.ds(0, 3), :, :, E_COLS[i]], ("e", i))
        left(pay_d.at[pl.ds(0, 3), :, :, D_COLS[i]], ("d", i))
        left(tot_e.at[pl.ds(0, 3), :, E_COLS[i]], ("e", "last", i))
        left(tot_d.at[pl.ds(0, 3), :, D_COLS[i]], ("d", "last", i))
    assert (len(sems.names), len(kinds.names)) == (N_ARRIVE, N_LEAVE)


def store(*refs):
    sources, results, sem = refs[:4], refs[4:8], refs[8]
    copies = [pltpu.make_async_copy(a, b, sem.at[i]) for i, (a, b) in enumerate(zip(sources, results))]
    for cp in copies:
        cp.start()
    for cp in copies:
        cp.wait()


def per_device(acts, dec_bias, enc_weight, enc_bias, dec_weight):
    vmem, anywhere = pl.BlockSpec(memory_space=pltpu.VMEM), pl.BlockSpec(memory_space=pl.ANY)
    results = (((ROWS, D), BF16), ((OWN, D), F32), ((OWN, D), F32), ((1, OWN), F32))
    in_vmem = pl.pallas_call(
        kernel,
        name="step",
        out_shape=tuple(pltpu.VMEM(*r) for r in results),
        in_specs=[anywhere] * 5,
        out_specs=(vmem,) * 4,
        scratch_shapes=[
            pltpu.VMEM((ROWS, D), F32),
            pltpu.VMEM((1, D), F32),
            pltpu.VMEM((1, OWN), BF16),
            pltpu.VMEM((OWN, D), BF16),
            pltpu.VMEM((2, NZ, 2, CH, D), BF16),
            pltpu.VMEM((SIDE, SIDE, OWN, WE), BF16),
            pltpu.VMEM((SIDE, SIDE, OWN, D), BF16),
            pltpu.VMEM((2, SIDE, 2, SUB, LAT), BF16),
            pltpu.VMEM((2, SIDE, LAT, PORTION), BF16),
            pltpu.VMEM((2, NZ, CH, D), F32),
            pltpu.VMEM((2, NZ, CH, D), BF16),
            pltpu.VMEM((2, NZ, CH, D), BF16),
            pltpu.VMEM((2, NZ, CH, D), BF16),
            pltpu.VMEM((2, 4, CH, D), BF16),
            pltpu.VMEM((2, 4, CH, D), BF16),
            pltpu.VMEM((2, NZ, 2, CH, D), BF16),
            pltpu.VMEM((LAT, D), F32),
            pltpu.VMEM((LAT, D), F32),
            pltpu.VMEM((LAT, 128), F32),
            pltpu.VMEM((LAT, 128), F32),
            pltpu.VMEM((SIDE, SIDE, OWN, GE), BF16),
            pltpu.VMEM((SIDE, SIDE, OWN, D), BF16),
            pltpu.VMEM((2, 2, OWN, GE), BF16),
            pltpu.VMEM((2, SIDE, OWN, GE), BF16),
            pltpu.VMEM((SIDE, OWN, GE), BF16),
            pltpu.VMEM((3, OWN, GE), BF16),
            pltpu.VMEM((2, 2, OWN, D), BF16),
            pltpu.VMEM((2, SIDE, OWN, D), BF16),
            pltpu.VMEM((SIDE, OWN, D), BF16),
            pltpu.VMEM((3, OWN, D), BF16),
            pltpu.VMEM((ROWS, D), BF16),
            pltpu.SemaphoreType.DMA((5,)),
            pltpu.SemaphoreType.DMA((N_LEAVE,)),
            pltpu.SemaphoreType.DMA((N_ARRIVE,)),
        ],
        compiler_params=pltpu.CompilerParams(collective_id=0, has_side_effects=True, vmem_limit_bytes=60 << 20),
    )(acts, dec_bias[None, :], enc_weight, enc_bias[None, :], dec_weight)
    recon, genc, gdec, gbias = pl.pallas_call(
        store,
        name="store",
        out_shape=tuple(jax.ShapeDtypeStruct(*r) for r in results),
        in_specs=[vmem] * 4,
        out_specs=(anywhere,) * 4,
        scratch_shapes=[pltpu.SemaphoreType.DMA((4,))],
    )(*[pltpu.with_memory_space_constraint(r, pltpu.VMEM) for r in in_vmem])
    return recon, genc, gdec, gbias[0]


def solution(mesh):
    torus = Mesh(mesh.devices.reshape(2, 2, SIDE, SIDE, SIDE), AXES)
    wide = P(("y", "x", "h"), None)
    return jax.shard_map(
        per_device,
        mesh=torus,
        in_specs=(wide, P(), P(AXES, None), P(AXES), P(AXES, None)),
        out_specs=(wide, P(AXES, None), P(AXES, None), P(AXES)),
        check_vma=False,
    )
```

time: 108 us -> 102 us (0.944)
  Pallas kernels: 108 us -> 101 us
    pallas_call x1, Pallas kernels: 106 us -> 99.7 us  [per_device(): pl.pallas_call(kernel, name='step', out_shape=tuple((pltpu.VMEM(*r) for r...]
where the time goes in v4:
time: 102 us; the launch traced here: 101 us
  Pallas kernels  101 us (99%)
    pallas_call x1, Pallas kernels, per_device(): pl.pallas_call(kernel, name='step', out_shape=tuple((pltpu.VMEM(*r) for r...  99.7 us

profile of v4, /device:TPU:1, one launch (start us, length us, event | category | flops | bytes accessed | tf_op | source)
XLA Modules:
  0.0 101.4 jit_solution(14267351835808924475)
XLA Ops:
  0.6 99.7 %step.1 = (bf16[256,2048]{1,0:T(8,128)(2,1)S(1)}, f32[16,2048]{1,0:T(8,128)S(1)}, f32[16,2048]{1,0:T(8,128)S(1)}, f32[1,16]{1,0:T(1,128)S(1)}) custom-call(f32[256,2048]{1,0:T(8,128)} %acts_hbm.1, f32[1,2048]{1,0:T(1,128)} %bitcast.3, bf16[16,2048]{1,0:T(8,128)(2,1)} %enc_hbm.1, bf16[1,16]{1,0:T(2,128)(2,1)} %bitcast.4, bf16[16,2048]{1,0:T(8,128)(2,1)} %dec_hbm.1), custom_call_target="tpu_custom_call" | custom-call | tf_op jit(solution)/shard_map/step/pallas_call | solution.py:456
  100.4 1.1 %store.1 = (bf16[256,2048]{1,0:T(8,128)(2,1)}, f32[16,2048]{1,0:T(8,128)}, f32[16,2048]{1,0:T(8,128)}, f32[1,16]{1,0:T(1,128)}) custom-call(bf16[256,2048]{1,0:T(8,128)(2,1)S(1)} %get-tuple-element.12.refs_0_, f32[16,2048]{1,0:T(8,128)S(1)} %get-tuple-element.13.refs_1_, f32[16,2048]{1,0:T(8,128)S(1)} %get-tuple-element.14.refs_2_, ...), custom_call_target="tpu_custom_call" | custom-call | tf_op jit(solution)/shard_map/store/pallas_call | solution.py:500

commit v5 on v4

--- a/solution.py
+++ b/solution.py
@@ -30,7 +30,7 @@
         return self.names.setdefault(name, len(self.names))
 
 
-N_ARRIVE, N_LEAVE = 104, 18
+N_ARRIVE, N_LEAVE = 105, 18
 NT = (((1,), (1,)), ((), ()))
 
 
@@ -249,6 +249,11 @@
     steps(0, 1, 2)
     decode(1, early)
     relay_acts("b", 2, 1)
+    norms = []
+    for q in range(2):
+        rows_q = wdec[2 * q : 2 * q + 2].reshape(LAT // 2, D).astype(F32)
+        norms.append(jnp.sqrt(jnp.sum(rows_q * rows_q, axis=1, keepdims=True) + 1e-06))
+    norms = jnp.concatenate(norms, axis=0)
     from_partner("late", 1)
     encode(1, late)
     decode(1, late)
@@ -275,16 +280,10 @@
             mine = rows(err, z, k).at[strip(r)]
             send(mine, mine, sems("gp", 0, k, r), at_z(1), "err")
             send(mine, mine, sems("gm", 0, k, r), at_z(-1), "err")
-            send(mine, mine, sems("errc", 0), partner, "errc")
+            send(mine, mine, sems("errc", 0, 0), partner, "errc")
 
     at_home(0)
     steps(1, 5, 6, 7)
-
-    norms = []
-    for q in range(2):
-        rows_q = wdec[2 * q : 2 * q + 2].reshape(LAT // 2, D).astype(F32)
-        norms.append(jnp.sqrt(jnp.sum(rows_q * rows_q, axis=1, keepdims=True) + 1e-06))
-    norms = jnp.concatenate(norms, axis=0)
 
     def incoming(s, k, r, sign, core=None):
         return rows(err, wrap(z - sign * (s + 1), NZ), k, core).at[strip(r)]
@@ -298,18 +297,19 @@
                 arrive(part, sems(name, s, k, r))
                 if s < 2 or (s == 2 and farthest(sign, r)):
                     send(part, part, sems(name, s + 1, k, r), at_z(sign), "err")
-                send(part, part, sems("errc", s), partner, "errc")
-
-    def err_from_partner(s):
-        arrive(err.at[0, pl.ds(0, (3, 2, 2, 1)[s])], sems("errc", s))
-
-    def backward(b, first, last):
-        block = err[:, pl.ds(2 * b, 2)].reshape(ROWS, D)
+                send(part, part, sems("errc", s, k if s == 3 else 0), partner, "errc")
+
+    def err_from_partner(s, k=0):
+        arrive(err.at[0, 0, 0] if s == 3 else err.at[0, pl.ds(0, (3, 2, 2)[s])], sems("errc", s, k))
+
+    def backward(b, first, last, half=None):
+        ks, n = (slice(None), ROWS) if half is None else (pl.ds(half, 1), PORTION)
+        block = err[ks, pl.ds(2 * b, 2)].reshape(n, D)
         weights = wdec[...].reshape(LAT, D)
         back = lax.dot_general(weights, block, NT, preferred_element_type=F32)
-        kept = jnp.concatenate([codes_t[0, b], codes_t[1, b]], axis=1)
+        kept = jnp.concatenate([codes_t[0, b], codes_t[1, b]], axis=1) if half is None else codes_t[half, b]
         grad_pre = jnp.where(kept.astype(F32) > 0.0, back + SPARSITY * norms, 0.0)
-        folded = grad_pre[:, :128] + grad_pre[:, 128:]
+        folded = grad_pre[:, :128] + grad_pre[:, 128:] if half is None else grad_pre
         gb[...] = folded if first else gb[...] + folded
         grad_bf = grad_pre.astype(BF16)
         if last:
@@ -317,7 +317,7 @@
             pay_e[:, :, :, 128:STATS] = cs[...].astype(BF16).reshape(SIDE, SIDE, OWN, 128)
         for left, data, acc, pay in ((grad_bf, cent, acc_e, pay_e), (kept, err, acc_d, pay_d)):
             for t in range(0, D, TILE):
-                right = data[:, pl.ds(2 * b, 2), :, :, t : t + TILE].reshape(ROWS, TILE)
+                right = data[ks, pl.ds(2 * b, 2), :, :, t : t + TILE].reshape(n, TILE)
                 total = jnp.dot(left, right, preferred_element_type=F32)
                 if not first:
                     total = total + acc[:, t : t + TILE]
@@ -390,12 +390,14 @@
     relay_err(2, 1)
     err_from_partner(2)
     backward(blocks[2], False, False)
+    err_from_partner(3, 0)
+    backward(blocks[3], False, False, 0)
     relay_err(3, 1)
     own_rec = rec.at[pl.ds(pl.multiple_of(own_rows, SUB), SUB)]
     send(own_rec, own_rec, sems("rc"), partner, "rec")
     send(own_rec, own_rec, sems("rz"), pair, "rec")
-    err_from_partner(3)
-    backward(blocks[3], False, True)
+    err_from_partner(3, 1)
+    backward(blocks[3], False, True, 1)
 
     for i in range(2):
         forward_sum(i, E_COLS[i], e_part, y, e_far, e_near, "e", at_y)

time: 102 us -> 101 us (level)
  no operation moved by 1% of the time
where the time goes in v5:
time: 101 us
  Pallas kernels  100 us (99%)
    pallas_call x1, Pallas kernels, per_device(): pl.pallas_call(kernel, name='step', out_shape=tuple((pltpu.VMEM(*r) for r...  99.4 us

profile of v5, /device:TPU:1, one launch (start us, length us, event | category | flops | bytes accessed | tf_op | source)
XLA Modules:
  0.0 101.1 jit_solution(5376700103796871376)
XLA Ops:
  0.6 99.4 %step.1 = (bf16[256,2048]{1,0:T(8,128)(2,1)S(1)}, f32[16,2048]{1,0:T(8,128)S(1)}, f32[16,2048]{1,0:T(8,128)S(1)}, f32[1,16]{1,0:T(1,128)S(1)}) custom-call(f32[256,2048]{1,0:T(8,128)} %acts_hbm.1, f32[1,2048]{1,0:T(1,128)} %bitcast.3, bf16[16,2048]{1,0:T(8,128)(2,1)} %enc_hbm.1, bf16[1,16]{1,0:T(2,128)(2,1)} %bitcast.4, bf16[16,2048]{1,0:T(8,128)(2,1)} %dec_hbm.1), custom_call_target="tpu_custom_call" | custom-call | tf_op jit(solution)/shard_map/step/pallas_call | solution.py:458
  100.0 1.1 %store.1 = (bf16[256,2048]{1,0:T(8,128)(2,1)}, f32[16,2048]{1,0:T(8,128)}, f32[16,2048]{1,0:T(8,128)}, f32[1,16]{1,0:T(1,128)}) custom-call(bf16[256,2048]{1,0:T(8,128)(2,1)S(1)} %get-tuple-element.12.refs_0_, f32[16,2048]{1,0:T(8,128)S(1)} %get-tuple-element.13.refs_1_, f32[16,2048]{1,0:T(8,128)S(1)} %get-tuple-element.14.refs_2_, ...), custom_call_target="tpu_custom_call" | custom-call | tf_op jit(solution)/shard_map/store/pallas_call | solution.py:502

commit v6 on v5

--- a/solution.py
+++ b/solution.py
@@ -384,10 +384,10 @@
     relay_err(1, 1)
     err_from_partner(0)
     backward(blocks[0], True, False)
+    relay_err(2, 1)
     relay_err(3, 0)
     err_from_partner(1)
     backward(blocks[1], False, False)
-    relay_err(2, 1)
     err_from_partner(2)
     backward(blocks[2], False, False)
     err_from_partner(3, 0)

time: 101 us -> 104 us (1.030)
  Pallas kernels: 100 us -> 103 us
    pallas_call x1, Pallas kernels: 99.4 us -> 102 us  [per_device(): pl.pallas_call(kernel, name='step', out_shape=tuple((pltpu.VMEM(*r) for r...]
where the time goes in v6:
time: 104 us; the launch traced here: 103 us
  Pallas kernels  103 us (99%)
    pallas_call x1, Pallas kernels, per_device(): pl.pallas_call(kernel, name='step', out_shape=tuple((pltpu.VMEM(*r) for r...  102 us

profile of v6, /device:TPU:1, one launch (start us, length us, event | category | flops | bytes accessed | tf_op | source)
XLA Modules:
  0.0 103.5 jit_solution(729806658721514044)
XLA Ops:
  0.6 101.8 %step.1 = (bf16[256,2048]{1,0:T(8,128)(2,1)S(1)}, f32[16,2048]{1,0:T(8,128)S(1)}, f32[16,2048]{1,0:T(8,128)S(1)}, f32[1,16]{1,0:T(1,128)S(1)}) custom-call(f32[256,2048]{1,0:T(8,128)} %acts_hbm.1, f32[1,2048]{1,0:T(1,128)} %bitcast.3, bf16[16,2048]{1,0:T(8,128)(2,1)} %enc_hbm.1, bf16[1,16]{1,0:T(2,128)(2,1)} %bitcast.4, bf16[16,2048]{1,0:T(8,128)(2,1)} %dec_hbm.1), custom_call_target="tpu_custom_call" | custom-call | tf_op jit(solution)/shard_map/step/pallas_call | solution.py:458
  102.4 1.1 %store.1 = (bf16[256,2048]{1,0:T(8,128)(2,1)}, f32[16,2048]{1,0:T(8,128)}, f32[16,2048]{1,0:T(8,128)}, f32[1,16]{1,0:T(1,128)}) custom-call(bf16[256,2048]{1,0:T(8,128)(2,1)S(1)} %get-tuple-element.12.refs_0_, f32[16,2048]{1,0:T(8,128)S(1)} %get-tuple-element.13.refs_1_, f32[16,2048]{1,0:T(8,128)S(1)} %get-tuple-element.14.refs_2_, ...), custom_call_target="tpu_custom_call" | custom-call | tf_op jit(solution)/shard_map/store/pallas_call | solution.py:502
